TPU v7x, 32 devices: a whole 2x2x4 slice. The times are simulated.
32 devices in a mesh: gx: 8 (over y, x, core), gy: 4 (over z).
Axes of the slice: x: 2, y: 2, z: 4, core: 2. Of those that a mesh axis runs over, the one named last changes fastest.
Arguments:
- adjoint_source: float32 [4, 64, 256, 512], P(None, 'gx', 'gy'), may hold values from -40 to 40, as said below
- conductivity: float32 [64, 256, 512], P('gx', 'gy'), may hold values from 0.1 to 10
- electrodes: int32 [4], replicated, may hold values from 0 to 16383
Outputs:
- solution_field: float32 [4, 64, 256, 512], P(None, 'gx', 'gy')
- residual: float32 [4, 64, 256, 512], P(None, 'gx', 'gy')
Inputs may be any that keep to these rules, and one draw needn't show every extreme that they name: `electrodes`: each entry is a surface cell index, its first coordinate times 256 plus its second. `adjoint_source`: drawn afresh cell by cell.
All inputs are finite; a program needn't handle non-finite values.
Results may differ from a plain program's by a relative error of at most 0.0003.
Values sent between devices are 32-bit elements; how exact they have to be, the bound alone decides.
A program may use at most 128 MiB of HBM per device.

v0:
```python
import functools
import math

import jax
import jax.numpy as jnp
from jax import lax
from jax.experimental import pallas as pl
from jax.experimental.pallas import tpu as pltpu
from jax.sharding import PartitionSpec as P

MESH = pl.DeviceIdType.MESH
F = 4
PAIRS = [(i, j) for i in range(F) for j in range(i, F)]
NP = len(PAIRS)
TILE = 8
GRANT_A = 15 * 1024 * 1024
GRANT_B = 5 * 1024 * 1024
LANES = 128


def remote(src, dst, send, recv, axis, index):
    return pltpu.make_async_remote_copy(
        src_ref=src, dst_ref=dst, send_sem=send, recv_sem=recv,
        device_id={axis: index}, device_id_type=MESH,
    )


def operator_kernel(
    nx, ny, current, adj, sig, elec, R, Q, W, sums,
    S, wt, edge, got, acc, part_x, part_y,
    local, xs, xr, ys, yr, ax_s, ax_r, ay_s, ay_r,
):
    cx, cy, cz = sig.shape
    total_y = ny * cy
    mx, my = lax.axis_index("gx"), lax.axis_index("gy")
    barrier = pltpu.get_barrier_semaphore()
    rows = pl.ds(TILE, cy)

    load_r = pltpu.make_async_copy(adj, R.at[:, pl.ds(1, cx), rows, :], local.at[0])
    load_s = pltpu.make_async_copy(sig, S.at[pl.ds(1, cx), rows, :], local.at[1])
    load_r.start()
    load_s.start()
    for axis, me, n in (("gx", mx, nx), ("gy", my, ny)):
        for d in range(1, n):
            pl.semaphore_signal(
                barrier, inc=1, device_id={axis: lax.rem(me + d, n)}, device_id_type=MESH
            )
    pl.semaphore_wait(barrier, nx + ny - 2)

    has_lo, has_hi = mx > 0, mx < nx - 1
    below, above = jnp.maximum(mx - 1, 0), jnp.minimum(mx + 1, nx - 1)
    y_lo, y_hi = my > 0, my < ny - 1
    left, right = jnp.maximum(my - 1, 0), jnp.minimum(my + 1, ny - 1)

    up_s = remote(sig.at[cx - 1], S.at[0, rows, :], xs.at[0], xr.at[0], "gx", above)
    dn_s = remote(sig.at[0], S.at[cx + 1, rows, :], xs.at[1], xr.at[1], "gx", below)
    up_r = remote(adj.at[:, cx - 1], R.at[:, 0, rows, :], xs.at[2], xr.at[2], "gx", above)
    dn_r = remote(adj.at[:, 0], R.at[:, cx + 1, rows, :], xs.at[3], xr.at[3], "gx", below)
    up_q = remote(Q.at[:, cx, rows, :], Q.at[:, 0, rows, :], xs.at[4], xr.at[4], "gx", above)
    dn_q = remote(Q.at[:, 1, rows, :], Q.at[:, cx + 1, rows, :], xs.at[5], xr.at[5], "gx", below)
    y_up = remote(edge.at[0], got.at[0], ys.at[0], yr.at[0], "gy", right)
    y_dn = remote(edge.at[1], got.at[1], ys.at[1], yr.at[1], "gy", left)
    y_up_q = remote(edge.at[2, pl.ds(0, F)], got.at[2, pl.ds(0, F)], ys.at[2], yr.at[2], "gy", right)
    y_dn_q = remote(edge.at[3, pl.ds(0, F)], got.at[3, pl.ds(0, F)], ys.at[3], yr.at[3], "gy", left)

    @pl.when(has_hi)
    def _():
        up_s.start()
        up_r.start()

    @pl.when(has_lo)
    def _():
        dn_s.start()
        dn_r.start()

    acc[...] = jnp.zeros_like(acc)
    edge_plane = jnp.zeros((cy, cz), jnp.float32)

    @pl.when(jnp.logical_not(has_lo))
    def _():
        S[0, rows, :] = edge_plane
        for f in range(F):
            R[f, 0, rows, :] = edge_plane
            Q[f, 0, rows, :] = edge_plane

    @pl.when(jnp.logical_not(has_hi))
    def _():
        S[cx + 1, rows, :] = edge_plane
        for f in range(F):
            R[f, cx + 1, rows, :] = edge_plane
            Q[f, cx + 1, rows, :] = edge_plane

    @pl.when(jnp.logical_not(y_lo))
    def _():
        got[0] = jnp.zeros(got.shape[1:], jnp.float32)
        got[2] = jnp.zeros(got.shape[1:], jnp.float32)

    @pl.when(jnp.logical_not(y_hi))
    def _():
        got[1] = jnp.zeros(got.shape[1:], jnp.float32)
        got[3] = jnp.zeros(got.shape[1:], jnp.float32)

    row_id = lax.broadcasted_iota(jnp.int32, (cy, LANES), 0)
    first = lax.broadcasted_iota(jnp.int32, (cy, LANES), 1) == 0

    def spike(x):
        cell = row_id + ((mx * cx + x - 1) * total_y + my * cy)
        for f in range(F):
            here = jnp.where(first & (cell == elec[f]), current, 0.0)
            R[f, x, rows, pl.ds(0, LANES)] = R[f, x, rows, pl.ds(0, LANES)] + here

    def pack(src, fields, base):
        def one(x, c):
            for k, ref in enumerate(src(x)):
                edge[base, k, pl.ds(x, 1), :] = ref(TILE + cy - 1)
                edge[base + 1, k, pl.ds(x, 1), :] = ref(TILE)
            return c
        lax.fori_loop(0, cx, one, 0)

    def row_r(f, x):
        return lambda y: R[f, x + 1, pl.ds(y, 1), :]

    def row_q(f, x):
        return lambda y: Q[f, x + 1, pl.ds(y, 1), :]

    def row_s(x):
        return lambda y: S[x + 1, pl.ds(y, 1), :]

    load_r.wait()

    def spike_loop(x, c):
        spike(x)
        return c

    lax.fori_loop(1, cx + 1, spike_loop, 0)
    load_s.wait()
    pack(lambda x: [row_r(f, x) for f in range(F)] + [row_s(x)], F + 1, 0)

    @pl.when(y_hi)
    def _():
        y_up.start()

    @pl.when(y_lo)
    def _():
        y_dn.start()

    @pl.when(y_lo)
    def _():
        y_up.wait_recv()

    @pl.when(y_hi)
    def _():
        y_dn.wait_recv()

    def unpack_first(x, c):
        for slot, y in ((0, TILE - 1), (1, TILE + cy)):
            for f in range(F):
                R[f, x + 1, pl.ds(y, 1), :] = got[slot, f, pl.ds(x, 1), :]
            S[x + 1, pl.ds(y, 1), :] = got[slot, F, pl.ds(x, 1), :]
        return c

    lax.fori_loop(0, cx, unpack_first, 0)

    lane = lax.broadcasted_iota(jnp.int32, (TILE, cz), 1)

    def add_grams(base, lefts, rights):
        for k, (i, j) in enumerate(PAIRS):
            prod = lefts[i] * rights[j]
            total = prod[:, :LANES]
            for c in range(LANES, cz, LANES):
                total = total + prod[:, c:c + LANES]
            acc[base + k] = acc[base + k] + total

    def apply(src, f, x, y, weights):
        mid = src[f, x, pl.ds(y, TILE), :]
        diag, xm, xp, ym, yp, zm, zp = weights
        out = diag * mid
        out = out - xm * src[f, x - 1, pl.ds(y, TILE), :]
        out = out - xp * src[f, x + 1, pl.ds(y, TILE), :]
        out = out - ym * src[f, x, pl.ds(y - 1, TILE), :]
        out = out - yp * src[f, x, pl.ds(y + 1, TILE), :]
        out = out - zm * pltpu.roll(mid, 1, axis=1)
        out = out - zp * pltpu.roll(mid, cz - 1, axis=1)
        return mid, out

    def first_plane(x):
        for t in range(cy // TILE):
            y = TILE + t * TILE
            here = S[x, pl.ds(y, TILE), :]
            others = (
                S[x - 1, pl.ds(y, TILE), :],
                S[x + 1, pl.ds(y, TILE), :],
                S[x, pl.ds(y - 1, TILE), :],
                S[x, pl.ds(y + 1, TILE), :],
                jnp.where(lane == 0, 0.0, pltpu.roll(here, 1, axis=1)),
                jnp.where(lane == cz - 1, 0.0, pltpu.roll(here, cz - 1, axis=1)),
            )
            diag = jnp.zeros_like(here)
            weights = []
            for other in others:
                inside = other > 0.0
                mean = 0.5 * (here + other)
                diag = diag + jnp.where(inside, mean, here)
                weights.append(jnp.where(inside, mean, 0.0))
            weights = [diag] + weights
            for k in range(7):
                wt[k, x - 1, pl.ds(t * TILE, TILE), :] = weights[k]
            rs, qs = [], []
            for f in range(F):
                mid, out = apply(R, f, x, y, weights)
                Q[f, x, pl.ds(y, TILE), :] = out
                rs.append(mid)
                qs.append(out)
            add_grams(0, rs, rs)
            add_grams(NP, rs, qs)

    def second_plane(x):
        for t in range(cy // TILE):
            y = TILE + t * TILE
            weights = [wt[k, x - 1, pl.ds(t * TILE, TILE), :] for k in range(7)]
            qs, ws = [], []
            for f in range(F):
                mid, out = apply(Q, f, x, y, weights)
                W[f, x - 1, pl.ds(t * TILE, TILE), :] = out
                qs.append(mid)
                ws.append(out)
            add_grams(2 * NP, qs, qs)
            add_grams(3 * NP, qs, ws)

    def run(plane):
        def one(x, c):
            plane(x)
            return c
        return one

    lax.fori_loop(2, cx, run(first_plane), 0)

    @pl.when(has_lo)
    def _():
        up_s.wait_recv()
        up_r.wait_recv()

    @pl.when(has_hi)
    def _():
        dn_s.wait_recv()
        dn_r.wait_recv()

    def ends(plane):
        def one(k, c):
            plane(k)
            return c
        return one

    lax.fori_loop(0, 2, ends(lambda k: spike(k * (cx + 1))), 0)
    lax.fori_loop(0, 2, ends(lambda k: first_plane(1 + k * (cx - 1))), 0)

    @pl.when(has_hi)
    def _():
        up_q.start()

    @pl.when(has_lo)
    def _():
        dn_q.start()

    pack(lambda x: [row_q(f, x) for f in range(F)], F, 2)

    @pl.when(y_hi)
    def _():
        y_up_q.start()

    @pl.when(y_lo)
    def _():
        y_dn_q.start()

    @pl.when(y_lo)
    def _():
        y_up_q.wait_recv()

    @pl.when(y_hi)
    def _():
        y_dn_q.wait_recv()

    def unpack_second(x, c):
        for slot, y in ((2, TILE - 1), (3, TILE + cy)):
            for f in range(F):
                Q[f, x + 1, pl.ds(y, 1), :] = got[slot, f, pl.ds(x, 1), :]
        return c

    lax.fori_loop(0, cx, unpack_second, 0)
    lax.fori_loop(2, cx, run(second_plane), 0)

    @pl.when(has_lo)
    def _():
        up_q.wait_recv()

    @pl.when(has_hi)
    def _():
        dn_q.wait_recv()

    lax.fori_loop(0, 2, ends(lambda k: second_plane(1 + k * (cx - 1))), 0)

    part_x[mx] = jnp.sum(acc[...], axis=1)

    def exchange(buf, axis, me, n, sends, recvs):
        copies = [
            remote(buf.at[me], buf.at[me], sends.at[d - 1], recvs.at[d - 1], axis, lax.rem(me + d, n))
            for d in range(1, n)
        ]
        for copy in copies:
            copy.start()
        for d in range(1, n):
            src = lax.rem(me + n - d, n)
            remote(
                buf.at[me], buf.at[src], sends.at[d - 1], recvs.at[d - 1], axis, src
            ).wait_recv()
        total = buf[0]
        for k in range(1, n):
            total = total + buf[k]
        return copies, total

    copies_x, total_x = exchange(part_x, "gx", mx, nx, ax_s, ax_r)
    part_y[my] = total_x
    copies_y, total = exchange(part_y, "gy", my, ny, ay_s, ay_r)
    sums[...] = jnp.broadcast_to(jnp.sum(total, axis=1, keepdims=True), sums.shape)

    for copy in copies_x + copies_y:
        copy.wait_send()

    @pl.when(has_hi)
    def _():
        up_s.wait_send()
        up_r.wait_send()
        up_q.wait_send()

    @pl.when(has_lo)
    def _():
        dn_s.wait_send()
        dn_r.wait_send()
        dn_q.wait_send()

    @pl.when(y_hi)
    def _():
        y_up.wait_send()
        y_up_q.wait_send()

    @pl.when(y_lo)
    def _():
        y_dn.wait_send()
        y_dn_q.wait_send()


def mat(a, b):
    return [
        [sum(a[i][k] * b[k][j] for k in range(1, F)) + a[i][0] * b[0][j] for j in range(F)]
        for i in range(F)
    ]


def add(a, b):
    return [[a[i][j] + b[i][j] for j in range(F)] for i in range(F)]


def sub(a, b):
    return [[a[i][j] - b[i][j] for j in range(F)] for i in range(F)]


def turn(a):
    return [[a[j][i] for j in range(F)] for i in range(F)]


def spd_solve(a, b):
    low = [[None] * F for _ in range(F)]
    inv = [None] * F
    rest = [list(row) for row in a]
    for k in range(F):
        inv[k] = 1.0 / rest[k][k]
        for i in range(k + 1, F):
            low[i][k] = rest[i][k] * inv[k]
        for i in range(k + 1, F):
            for j in range(k + 1, i + 1):
                rest[i][j] = rest[i][j] - low[i][k] * rest[j][k]
    out = [list(row) for row in b]
    for i in range(F):
        for k in range(i):
            out[i] = [u - low[i][k] * v for u, v in zip(out[i], out[k])]
    out = [[u * inv[i] for u in out[i]] for i in range(F)]
    for i in reversed(range(F)):
        for k in range(i + 1, F):
            out[i] = [u - low[k][i] * v for u, v in zip(out[i], out[k])]
    return out


def finish_kernel(sums, r_ref, q_ref, w_ref, x_ref, e_ref, coef):
    @pl.when(pl.program_id(0) == 0)
    def _():
        grams = []
        for g in range(4):
            m = [[None] * F for _ in range(F)]
            for k, (i, j) in enumerate(PAIRS):
                m[i][j] = m[j][i] = sums[pl.ds(g * NP + k, 1), :]
            grams.append(m)
        s0, s1, s2, s3 = grams
        a0 = spd_solve(s1, s0)
        s1a, s2a = mat(s1, a0), mat(s2, a0)
        a0t = turn(a0)
        rr = add(sub(sub(s0, s1a), turn(s1a)), mat(a0t, s2a))
        cross = add(sub(sub(s1, s2a), turn(s2a)), mat(a0t, mat(s3, a0)))
        beta = spd_solve(s0, rr)
        curve = sub(cross, mat(turn(beta), mat(s1, beta)))
        a1 = spd_solve(curve, rr)
        m1 = add(add(a0, a1), mat(beta, a1))
        m2 = mat(a0, a1)
        for i in range(F):
            for j in range(F):
                coef[pl.ds(i * F + j, 1), :] = m1[i][j]
                coef[pl.ds(F * F + i * F + j, 1), :] = m2[i][j]

    x = pl.program_id(0)
    cy, cz = w_ref.shape[2:]
    c1 = [[jnp.broadcast_to(coef[pl.ds(i * F + j, 1), :], (TILE, LANES)) for j in range(F)] for i in range(F)]
    c2 = [[jnp.broadcast_to(coef[pl.ds(F * F + i * F + j, 1), :], (TILE, LANES)) for j in range(F)] for i in range(F)]

    def tile(t, c):
        y = pl.ds(pl.multiple_of(t * TILE, TILE), TILE)
        wide_y = pl.ds(pl.multiple_of(t * TILE + TILE, TILE), TILE)
        for z in range(0, cz, LANES):
            at = pl.ds(z, LANES)
            rs = [r_ref[f, x + 1, wide_y, at] for f in range(F)]
            qs = [q_ref[f, x + 1, wide_y, at] for f in range(F)]
            ws = [w_ref[f, x, y, at] for f in range(F)]
            for j in range(F):
                field = rs[0] * c1[0][j] - qs[0] * c2[0][j]
                left = rs[j] - qs[0] * c1[0][j] + ws[0] * c2[0][j]
                for i in range(1, F):
                    field = field + rs[i] * c1[i][j] - qs[i] * c2[i][j]
                    left = left - qs[i] * c1[i][j] + ws[i] * c2[i][j]
                x_ref[j, 0, y, at] = field
                e_ref[j, 0, y, at] = left
        return c

    lax.fori_loop(0, cy // TILE, tile, 0)


def shards(nx, ny, adj, sig, elec):
    cx, cy, cz = sig.shape
    current = math.sqrt(nx * cx * ny * cy * cz)
    block = jax.ShapeDtypeStruct(adj.shape, jnp.float32)
    hbm = pl.BlockSpec(memory_space=pltpu.HBM)
    vmem = pl.BlockSpec(memory_space=pltpu.VMEM)
    padded = (cx + 2, cy + 2 * TILE, cz)
    wide = jax.ShapeDtypeStruct((F,) + padded, jnp.float32)
    dma = pltpu.SemaphoreType.DMA
    adj = pltpu.with_memory_space_constraint(adj, pltpu.HBM)
    sig = pltpu.with_memory_space_constraint(sig, pltpu.HBM)
    r, q, w, sums = pl.pallas_call(
        functools.partial(operator_kernel, nx, ny, current),
        out_shape=(wide, wide, block, jax.ShapeDtypeStruct((4 * NP, LANES), jnp.float32)),
        in_specs=[hbm, hbm, pl.BlockSpec(memory_space=pltpu.SMEM)],
        out_specs=(vmem, vmem, vmem, vmem),
        scratch_shapes=[
            pltpu.VMEM(padded, jnp.float32),
            pltpu.VMEM((7, cx, cy, cz), jnp.float32),
            pltpu.VMEM((4, F + 1, cx, cz), jnp.float32),
            pltpu.VMEM((4, F + 1, cx, cz), jnp.float32),
            pltpu.VMEM((4 * NP, TILE, LANES), jnp.float32),
            pltpu.VMEM((nx, 4 * NP, LANES), jnp.float32),
            pltpu.VMEM((ny, 4 * NP, LANES), jnp.float32),
            dma((2,)), dma((6,)), dma((6,)), dma((4,)), dma((4,)),
            dma((max(nx - 1, 1),)), dma((max(nx - 1, 1),)),
            dma((max(ny - 1, 1),)), dma((max(ny - 1, 1),)),
        ],
        compiler_params=pltpu.CompilerParams(collective_id=0, has_side_effects=True, vmem_limit_bytes=GRANT_A),
    )(adj, sig, elec)
    slab = pl.BlockSpec((F, 1, cy, cz), lambda x: (0, x, 0, 0))
    return pl.pallas_call(
        finish_kernel,
        grid=(cx,),
        out_shape=(block, block),
        in_specs=[vmem, vmem, vmem, vmem],
        out_specs=(slab, slab),
        scratch_shapes=[pltpu.VMEM((2 * F * F, LANES), jnp.float32)],
        compiler_params=pltpu.CompilerParams(vmem_limit_bytes=GRANT_B),
    )(sums, r, q, w)


def solution(mesh):
    placed = (P(None, "gx", "gy", None), P("gx", "gy", None), P())
    return jax.shard_map(
        functools.partial(shards, mesh.shape["gx"], mesh.shape["gy"]),
        mesh=mesh,
        in_specs=placed,
        out_specs=(P(None, "gx", "gy", None), P(None, "gx", "gy", None)),
        check_vma=False,
    )
```

profile of v0, /device:TPU:0, one launch (start us, length us, event | category | flops | bytes accessed | tf_op | source)
XLA Modules:
  0.0 50.8 jit_solution(11639175689932945219)
XLA Ops:
  0.6 0.0 copy-start
  0.6 0.6 %copy-done = s32[4]{0:T(128)S(1)} copy-done((s32[4]{0:T(128)S(1)}, s32[4]{0:T(128)}, u32[]{:S(2)}) %copy-start) | copy-done | bytes 40
  1.3 42.1 %shard_map.50 = (f32[4,10,80,512]{3,2,1,0:T(8,128)S(1)}, f32[4,10,80,512]{3,2,1,0:T(8,128)S(1)}, f32[4,8,64,512]{3,2,1,0:T(8,128)S(1)}, f32[40,128]{1,0:T(8,128)S(1)}) custom-call(f32[4,8,64,512]{3,2,1,0:T(8,128)} %adj.1, f32[8,64,512]{2,1,0:T(8,128)} %sig.1, s32[4]{0:T(128)S(1)} %copy-done), custom_call_target="tpu_custom_call" | custom-call | tf_op jit(solution)/shard_map/pallas_call | solution.py:455
  43.4 7.4 %shard_map.51 = (f32[4,8,64,512]{3,2,1,0:T(8,128)}, f32[4,8,64,512]{3,2,1,0:T(8,128)}) custom-call(f32[40,128]{1,0:T(8,128)S(1)} %get-tuple-element.6.sums, f32[4,10,80,512]{3,2,1,0:T(8,128)S(1)} %get-tuple-element.7.r_ref, f32[4,10,80,512]{3,2,1,0:T(8,128)S(1)} %get-tuple-element.8.q_ref, f32[4,8,64,512]{3,2,1,0:T(8,128)S(1)} %get-tuple-element.9.w_ref), custom_call_target="tpu_custom_call" | custom-call | tf_op jit(solution)/shard_map/pallas_call | solution.py:475
Async XLA Ops:
  0.6 0.7 %copy-start = (s32[4]{0:T(128)S(1)}, s32[4]{0:T(128)}, u32[]{:S(2)}) copy-start(s32[4]{0:T(128)} %elec.1) | copy-start | bytes 52
where the time goes:
time: 50.9 us; the launch traced here: 50.8 us
  Pallas kernels  49.5 us (97%)
  local copies, waits for them, and re-layouts  0.65 us (1%)
  between operations  0.65 us (1%)
    pallas_call x1, Pallas kernels, shards(): pl.pallas_call(functools.partial(operator_kernel, nx, ny, current), out_s...  42.1 us
    pallas_call x1, Pallas kernels, shards(): pl.pallas_call(finish_kernel, grid=(cx,), out_shape=(block, block), in_sp...  7.39 us

commit v1 on v0

v1 whole, which is shorter than its diff:
```python
import functools
import math

import jax
import jax.numpy as jnp
from jax import lax
from jax.experimental import pallas as pl
from jax.experimental.pallas import tpu as pltpu
from jax.sharding import PartitionSpec as P

MESH = pl.DeviceIdType.MESH
F = 4
PAIRS = [(i, j) for i in range(F) for j in range(i, F)]
NP = len(PAIRS)
TILE = 8
GRANT_A = 16 * 1024 * 1024
GRANT_B = 5 * 1024 * 1024
LANES = 128


def remote(src, dst, send, recv, axis, index):
    return pltpu.make_async_remote_copy(
        src_ref=src, dst_ref=dst, send_sem=send, recv_sem=recv,
        device_id={axis: index}, device_id_type=MESH,
    )


def operator_kernel(
    nx, ny, current, adj, sig, elec, R, Q, W, sums,
    S, wt, qx, relay_r, relay_s, relay_q, acc, part_x, part_y,
    local, xs, xr, hr, fs, ys, yr, ax_s, ax_r, ay_s, ay_r,
):
    cx, cy, cz = sig.shape
    Z = cz // LANES
    T = cy // TILE
    total_y = ny * cy
    mx, my = lax.axis_index("gx"), lax.axis_index("gy")
    barrier = pltpu.get_barrier_semaphore()
    rows = pl.ds(TILE, cy)
    inner = pl.ds(1, cx)

    loads = []
    for z in range(Z):
        at = pl.ds(z * LANES, LANES)
        loads.append(pltpu.make_async_copy(adj.at[:, :, :, at], R.at[:, inner, z, rows, :], local.at[0, z]))
        loads.append(pltpu.make_async_copy(sig.at[:, :, at], S.at[inner, z, rows, :], local.at[1, z]))
    for load in loads:
        load.start()
    for axis, me, n in (("gx", mx, nx), ("gy", my, ny)):
        for d in range(1, n):
            pl.semaphore_signal(
                barrier, inc=1, device_id={axis: lax.rem(me + d, n)}, device_id_type=MESH
            )

    has_lo, has_hi = mx > 0, mx < nx - 1
    below, above = jnp.maximum(mx - 1, 0), jnp.minimum(mx + 1, nx - 1)
    y_lo, y_hi = my > 0, my < ny - 1
    left, right = jnp.maximum(my - 1, 0), jnp.minimum(my + 1, ny - 1)

    half = Z // 2
    mid = nx // 2
    relaying = nx >= 4
    order = [z for k in range(half) for z in (k, Z - 1 - k)] + ([half] if Z % 2 else [])
    first_up = [z for z in order if z < half]
    first_dn = [z for z in order if z >= half]
    by_relay = [z for k, z in enumerate(order) if relaying and (k // 2) % 2 == 1]
    slot = {z: k for k, z in enumerate(by_relay)}
    up_cross, dn_cross = mx == mid - 1, mx == mid
    up_end, dn_end = mx == nx - 1, mx == 0

    def lanes(z):
        return pl.ds(z * LANES, LANES)

    def hop(d, k, z, axis_to):
        plane = cx - 1 if d == 0 else 0
        halo = 0 if d == 0 else cx + 1
        if k == 0:
            src, dst = adj.at[:, plane, :, lanes(z)], R.at[:, halo, z, rows, :]
        elif k == 1:
            src, dst = sig.at[plane, :, lanes(z)], S.at[halo, z, rows, :]
        else:
            src, dst = Q.at[:, plane, z, rows, :], qx.at[d, :, z]
        return remote(src, dst, xs.at[d, k, z], xr.at[d, k, z], "gx", axis_to)

    def to_relay(d, k, z):
        plane = cx - 1 if d == 0 else 0
        end = nx - 1 if d == 0 else 0
        if k == 0:
            src = adj.at[:, plane, :, lanes(z)]
        elif k == 1:
            src = sig.at[plane, :, lanes(z)]
        else:
            src = Q.at[:, plane, z, rows, :]
        dst = (relay_r, relay_s, relay_q)[k].at[slot[z]]
        return remote(src, dst, xs.at[d, k, z], hr.at[k, slot[z]], "gx", end)

    def from_relay(d, k, z):
        halo = 0 if d == 0 else cx + 1
        if k == 0:
            dst = R.at[:, halo, z, rows, :]
        elif k == 1:
            dst = S.at[halo, z, rows, :]
        else:
            dst = qx.at[d, :, z]
        src = (relay_r, relay_s, relay_q)[k].at[slot[z]]
        target = mid if d == 0 else mid - 1
        return remote(src, dst, fs.at[k, slot[z]], xr.at[d, k, z], "gx", target)

    sides = ((0, has_hi, above, up_cross, up_end), (1, has_lo, below, dn_cross, dn_end))

    def send(d, k, z):
        _, there, to, cross, _ = sides[d]
        if z in by_relay:
            @pl.when(there & jnp.logical_not(cross))
            def _():
                hop(d, k, z, to).start()

            @pl.when(cross)
            def _():
                to_relay(d, k, z).start()
        else:
            @pl.when(there)
            def _():
                hop(d, k, z, to).start()

    def forward(d, k, z):
        @pl.when(sides[d][4])
        def _():
            to_relay(d, k, z).wait_recv()
            from_relay(d, k, z).start()

    def arrive(d, k, z):
        hop(d, k, z, above if d == 0 else below).wait_recv()

    def y_hop(d, k):
        src_row, dst_row = (TILE + cy - 1, TILE - 1) if d == 0 else (TILE, TILE + cy)
        to = right if d == 0 else left
        if k == 0:
            src, dst = R.at[:, inner, :, src_row, :], R.at[:, inner, :, dst_row, :]
        elif k == 1:
            src, dst = S.at[inner, :, src_row, :], S.at[inner, :, dst_row, :]
        elif k == 2:
            span = pl.ds(1, cx - 2)
            src, dst = Q.at[:, span, :, src_row, :], Q.at[:, span, :, dst_row, :]
        else:
            x = 0 if k == 3 else cx - 1
            src, dst = Q.at[:, x, :, src_row, :], Q.at[:, x, :, dst_row, :]
        return remote(src, dst, ys.at[d, k], yr.at[d, k], "gy", to)

    def y_send(kinds):
        for d, there in ((0, y_hi), (1, y_lo)):
            @pl.when(there)
            def _():
                for k in kinds:
                    y_hop(d, k).start()

    def y_arrive(kinds):
        for d, there in ((0, y_lo), (1, y_hi)):
            @pl.when(there)
            def _():
                for k in kinds:
                    y_hop(d, k).wait_recv()

    pl.semaphore_wait(barrier, nx + ny - 2)
    for z in order:
        for k in (0, 1):
            send(0, k, z)
            send(1, k, z)

    acc[...] = jnp.zeros_like(acc)
    nothing = jnp.zeros((cy, LANES), jnp.float32)
    no_row = jnp.zeros((1, LANES), jnp.float32)
    for load in loads:
        load.wait()

    row_id = lax.broadcasted_iota(jnp.int32, (cy, LANES), 0)
    first = lax.broadcasted_iota(jnp.int32, (cy, LANES), 1) == 0

    def spike(x):
        cell = row_id + ((mx * cx + x - 1) * total_y + my * cy)
        for f in range(F):
            here = jnp.where(first & (cell == elec[f]), current, 0.0)
            R[f, x, 0, rows, :] = R[f, x, 0, rows, :] + here

    def loop(lo, hi, body):
        def one(k, c):
            body(k)
            return c
        lax.fori_loop(lo, hi, one, 0)

    loop(1, cx + 1, spike)
    y_send((0, 1))

    for there, halo, own in ((has_lo, 0, 1), (has_hi, cx + 1, cx)):
        @pl.when(jnp.logical_not(there))
        def _():
            for z in range(Z):
                S[halo, z, rows, :] = S[own, z, rows, :]
                for f in range(F):
                    R[f, halo, z, rows, :] = nothing

    for there, halo, own in ((y_lo, TILE - 1, TILE), (y_hi, TILE + cy, TILE + cy - 1)):
        @pl.when(jnp.logical_not(there))
        def _():
            def fill(x):
                for z in range(Z):
                    S[x + 1, z, pl.ds(halo, 1), :] = S[x + 1, z, pl.ds(own, 1), :]
                    for f in range(F):
                        R[f, x + 1, z, pl.ds(halo, 1), :] = no_row
                        Q[f, x, z, pl.ds(halo, 1), :] = no_row
            loop(0, cx, fill)

    lane = lax.broadcasted_iota(jnp.int32, (TILE, LANES), 1)
    lane_lo, lane_hi = lane == 0, lane == LANES - 1

    def beside(get, zs, edge):
        blocks, fwd, bwd = {}, {}, {}
        for z in zs:
            for n in (z - 1, z, z + 1):
                if 0 <= n < Z and n not in blocks:
                    blocks[n] = get(n)
        for z in zs:
            for n in (z - 1, z):
                if n in blocks and n not in fwd:
                    fwd[n] = pltpu.roll(blocks[n], 1, axis=1)
            for n in (z, z + 1):
                if n in blocks and n not in bwd:
                    bwd[n] = pltpu.roll(blocks[n], LANES - 1, axis=1)
        out = {}
        for z in zs:
            before = fwd[z - 1] if z > 0 else edge(blocks[z])
            after = bwd[z + 1] if z < Z - 1 else edge(blocks[z])
            out[z] = (
                blocks[z],
                jnp.where(lane_lo, before, fwd[z]),
                jnp.where(lane_hi, after, bwd[z]),
            )
        return out

    def add_grams(base, lefts, rights):
        zs = list(lefts[0])
        for k, (i, j) in enumerate(PAIRS):
            total = None
            for z in zs:
                prod = lefts[i][z] * rights[j][z]
                total = prod if total is None else total + prod
            acc[base + k] = acc[base + k] + total

    def first_tile(x, t, zs):
        y = pl.multiple_of(t * TILE, TILE)
        at, up, dn = pl.ds(y + TILE, TILE), pl.ds(y + TILE - 1, TILE), pl.ds(y + TILE + 1, TILE)
        out_at = pl.ds(y, TILE)
        weights = {}
        near = beside(lambda z: S[x, z, at, :], zs, lambda v: v)
        for z in zs:
            here, zm, zp = near[z]
            faces = [
                here + S[x - 1, z, at, :], here + S[x + 1, z, at, :],
                here + S[x, z, up, :], here + S[x, z, dn, :], here + zm, here + zp,
            ]
            diag = ((faces[0] + faces[1]) + (faces[2] + faces[3])) + (faces[4] + faces[5])
            weights[z] = [diag] + faces
            for k in range(7):
                wt[k, x - 1, z, out_at, :] = weights[z][k]
        rs, qs = [], []
        for f in range(F):
            near = beside(lambda z: R[f, x, z, at, :], zs, jnp.zeros_like)
            r, q = {}, {}
            for z in zs:
                mid_v, zm, zp = near[z]
                d, wxm, wxp, wym, wyp, wzm, wzp = weights[z]
                out = d * mid_v - wzm * zm - wzp * zp
                out = out - wxm * R[f, x - 1, z, at, :] - wxp * R[f, x + 1, z, at, :]
                out = out - wym * R[f, x, z, up, :] - wyp * R[f, x, z, dn, :]
                Q[f, x - 1, z, at, :] = out
                r[z], q[z] = mid_v, out
            rs.append(r)
            qs.append(q)
        add_grams(0, rs, rs)
        add_grams(NP, rs, qs)

    def second_tile(x, t, zs, low, high):
        y = pl.multiple_of(t * TILE, TILE)
        at, up, dn = pl.ds(y + TILE, TILE), pl.ds(y + TILE - 1, TILE), pl.ds(y + TILE + 1, TILE)
        out_at = pl.ds(y, TILE)
        qs, ws = [], []
        for f in range(F):
            near = beside(lambda z: Q[f, x - 1, z, at, :], zs, jnp.zeros_like)
            q, w = {}, {}
            for z in zs:
                mid_v, zm, zp = near[z]
                out = wt[0, x - 1, z, out_at, :] * mid_v
                out = out - wt[5, x - 1, z, out_at, :] * zm - wt[6, x - 1, z, out_at, :] * zp
                if low:
                    out = out - wt[1, x - 1, z, out_at, :] * Q[f, x - 2, z, at, :]
                if high:
                    out = out - wt[2, x - 1, z, out_at, :] * Q[f, x, z, at, :]
                out = out - wt[3, x - 1, z, out_at, :] * Q[f, x - 1, z, up, :]
                out = out - wt[4, x - 1, z, out_at, :] * Q[f, x - 1, z, dn, :]
                W[f, x - 1, z, out_at, :] = out
                q[z], w[z] = mid_v, out
            qs.append(q)
            ws.append(w)
        add_grams(2 * NP, qs, qs)
        add_grams(3 * NP, qs, ws)

    def face_tile(d, z, t, grams):
        x = 0 if d == 0 else cx - 1
        y = pl.multiple_of(t * TILE, TILE)
        at, out_at = pl.ds(y + TILE, TILE), pl.ds(y, TILE)
        face = wt[1 + d, x, z, out_at, :]
        vs = [face * qx[d, f, z, out_at, :] for f in range(F)]
        for f in range(F):
            W[f, x, z, out_at, :] = W[f, x, z, out_at, :] - vs[f]
        if grams:
            qs = [Q[f, x, z, at, :] for f in range(F)]
            for k, (i, j) in enumerate(PAIRS):
                acc[3 * NP + k] = acc[3 * NP + k] - (qs[i] * vs[j] + vs[i] * qs[j])

    def face(d, z, grams):
        @pl.when((has_lo, has_hi)[d])
        def _():
            arrive(d, 2, z)
            loop(0, T, lambda t: face_tile(d, z, t, grams))

    every = list(range(Z))

    def middle(planes, tile, *rest):
        lo, hi = planes
        loop(lo, hi, lambda x: loop(1, T - 1, lambda t: tile(x, t, every, *rest)))

    def rims(planes, tile, *rest):
        lo, hi = planes
        loop(lo, hi, lambda x: loop(0, 2, lambda k: tile(x, k * (T - 1), every, *rest)))

    def chunk(z):
        for d, there in ((0, has_lo), (1, has_hi)):
            @pl.when(there)
            def _():
                arrive(d, 0, z)
                arrive(d, 1, z)
        if z == 0:
            loop(0, 2, lambda k: spike(k * (cx + 1)))
        loop(0, 2, lambda k: loop(0, T, lambda t: first_tile(1 + k * (cx - 1), t, [z])))

    def forward_all(k_list, zs):
        for z in zs:
            for d in (0, 1):
                for k in k_list:
                    if z in by_relay:
                        forward(d, k, z)

    split = (cx + 2) // 2
    middle((2, split), first_tile)
    y_arrive((0, 1))
    forward_all((0, 1), by_relay[:1])
    rims((2, cx), first_tile)
    forward_all((0, 1), by_relay[1:])
    middle((split, cx), first_tile)
    y_send((2,))

    sent_up = sent_dn = 0
    ready = set()

    def send_ready(d, limit):
        plan = (first_up + first_dn) if d == 0 else (first_dn + first_up)
        done = sent[d]
        while len(done) < limit and plan[len(done)] in ready:
            send(d, 2, plan[len(done)])
            done.append(plan[len(done)])

    sent = ([], [])
    for n, z in enumerate(order):
        chunk(z)
        ready.add(z)
        send_ready(0, Z)
        send_ready(1, Z)
        if n == 0:
            middle((3, cx - 1), second_tile, True, True)
        if n == 1:
            y_arrive((2,))
            rims((3, cx - 1), second_tile, True, True)
    y_send((3, 4))

    ends = lambda k: 2 + k * (cx - 3)
    loop(0, 2, lambda k: loop(0, T, lambda t: second_tile(ends(k), t, every, True, True)))
    middle((1, 2), second_tile, False, True)
    middle((cx, cx + 1), second_tile, True, False)
    y_arrive((3, 4))
    rims((1, 2), second_tile, False, True)
    rims((cx, cx + 1), second_tile, True, False)

    early = [(0, z) for z in first_up] + [(1, z) for z in first_dn]
    late = [(0, z) for z in first_dn] + [(1, z) for z in first_up]
    rank = {z: n for n, z in enumerate(order)}
    early.sort(key=lambda p: rank[p[1]])
    late.sort(key=lambda p: rank[p[1]])
    for d, z in early:
        if z in by_relay:
            forward(d, 2, z)
    for d, z in early:
        face(d, z, True)

    def compact(parts):
        lane_sum = jnp.sum(parts, axis=1, keepdims=True)
        out = jnp.zeros((TILE, LANES), jnp.float32)
        for k in range(4 * NP // TILE):
            out = jnp.where(lane == k, lane_sum[k * TILE:(k + 1) * TILE], out)
        return out

    part_x[mx] = compact(jnp.sum(acc[...], axis=1))

    def exchange(buf, axis, me, n, sends, recvs):
        copies = [
            remote(buf.at[me], buf.at[me], sends.at[d - 1], recvs.at[d - 1], axis, lax.rem(me + d, n))
            for d in range(1, n)
        ]
        for copy in copies:
            copy.start()
        return copies

    def gather(buf, axis, me, n, sends, recvs):
        for d in range(1, n):
            src = lax.rem(me + n - d, n)
            remote(
                buf.at[me], buf.at[src], sends.at[d - 1], recvs.at[d - 1], axis, src
            ).wait_recv()
        total = buf[0]
        for k in range(1, n):
            total = total + buf[k]
        return total

    copies_x = exchange(part_x, "gx", mx, nx, ax_s, ax_r)
    for d, z in late:
        if z in by_relay:
            forward(d, 2, z)
    cut = len(late) // 2
    for d, z in late[:cut]:
        face(d, z, False)
    part_y[my] = gather(part_x, "gx", mx, nx, ax_s, ax_r)
    copies_y = exchange(part_y, "gy", my, ny, ay_s, ay_r)
    for d, z in late[cut:]:
        face(d, z, False)
    sums[...] = gather(part_y, "gy", my, ny, ay_s, ay_r)

    for copy in copies_x + copies_y:
        copy.wait_send()
    for d in (0, 1):
        @pl.when(sides[d][1])
        def _():
            for z in order:
                for k in range(3):
                    hop(d, k, z, sides[d][2]).wait_send()

        @pl.when(sides[d][4])
        def _():
            for z in by_relay:
                for k in range(3):
                    from_relay(d, k, z).wait_send()
    for d, there in ((0, y_hi), (1, y_lo)):
        @pl.when(there)
        def _():
            for k in range(5):
                y_hop(d, k).wait_send()


def mat(a, b):
    return [
        [sum(a[i][k] * b[k][j] for k in range(1, F)) + a[i][0] * b[0][j] for j in range(F)]
        for i in range(F)
    ]


def add(a, b):
    return [[a[i][j] + b[i][j] for j in range(F)] for i in range(F)]


def sub(a, b):
    return [[a[i][j] - b[i][j] for j in range(F)] for i in range(F)]


def turn(a):
    return [[a[j][i] for j in range(F)] for i in range(F)]


def spd_solve(a, b):
    low = [[None] * F for _ in range(F)]
    inv = [None] * F
    rest = [list(row) for row in a]
    for k in range(F):
        inv[k] = 1.0 / rest[k][k]
        for i in range(k + 1, F):
            low[i][k] = rest[i][k] * inv[k]
        for i in range(k + 1, F):
            for j in range(k + 1, i + 1):
                rest[i][j] = rest[i][j] - low[i][k] * rest[j][k]
    out = [list(row) for row in b]
    for i in range(F):
        for k in range(i):
            out[i] = [u - low[i][k] * v for u, v in zip(out[i], out[k])]
    out = [[u * inv[i] for u in out[i]] for i in range(F)]
    for i in reversed(range(F)):
        for k in range(i + 1, F):
            out[i] = [u - low[k][i] * v for u, v in zip(out[i], out[k])]
    return out


def finish_kernel(sums, r_ref, q_ref, w_ref, x_ref, e_ref, coef):
    @pl.when(pl.program_id(0) == 0)
    def _():
        lane = lax.broadcasted_iota(jnp.int32, (TILE, LANES), 1)
        rows = []
        for k in range(4 * NP // TILE):
            column = jnp.sum(jnp.where(lane == k, sums[...], 0.0), axis=1, keepdims=True)
            wide = jnp.broadcast_to(column, (TILE, LANES))
            rows.extend(wide[s:s + 1] for s in range(TILE))
        grams = []
        for g in range(4):
            m = [[None] * F for _ in range(F)]
            for k, (i, j) in enumerate(PAIRS):
                m[i][j] = m[j][i] = rows[g * NP + k]
            grams.append(m)
        s0, s1, s2, s3 = grams
        a0 = spd_solve(s1, s0)
        s1a, s2a = mat(s1, a0), mat(s2, a0)
        a0t = turn(a0)
        rr = add(sub(sub(s0, s1a), turn(s1a)), mat(a0t, s2a))
        cross = add(sub(sub(s1, s2a), turn(s2a)), mat(a0t, mat(s3, a0)))
        beta = spd_solve(s0, rr)
        curve = sub(cross, mat(turn(beta), mat(s1, beta)))
        a1 = spd_solve(curve, rr)
        m1 = add(add(a0, a1), mat(beta, a1))
        m2 = mat(a0, a1)
        for i in range(F):
            for j in range(F):
                coef[pl.ds(i * F + j, 1), :] = m1[i][j]
                coef[pl.ds(F * F + i * F + j, 1), :] = m2[i][j]

    x = pl.program_id(0)
    cy = w_ref.shape[3]
    Z = w_ref.shape[2]
    c1 = [[jnp.broadcast_to(coef[pl.ds(i * F + j, 1), :], (TILE, LANES)) for j in range(F)] for i in range(F)]
    c2 = [[jnp.broadcast_to(coef[pl.ds(F * F + i * F + j, 1), :], (TILE, LANES)) for j in range(F)] for i in range(F)]

    def tile(t, c):
        y = pl.ds(pl.multiple_of(t * TILE, TILE), TILE)
        wide_y = pl.ds(pl.multiple_of(t * TILE + TILE, TILE), TILE)
        for z in range(Z):
            at = pl.ds(z * LANES, LANES)
            rs = [r_ref[f, x + 1, z, wide_y, :] for f in range(F)]
            qs = [q_ref[f, x, z, wide_y, :] for f in range(F)]
            ws = [w_ref[f, x, z, y, :] for f in range(F)]
            for j in range(F):
                field = rs[0] * c1[0][j] - qs[0] * c2[0][j]
                left = rs[j] - qs[0] * c1[0][j] + ws[0] * c2[0][j]
                for i in range(1, F):
                    field = field + rs[i] * c1[i][j] - qs[i] * c2[i][j]
                    left = left - qs[i] * c1[i][j] + ws[i] * c2[i][j]
                x_ref[j, 0, y, at] = field + field
                e_ref[j, 0, y, at] = left
        return c

    lax.fori_loop(0, cy // TILE, tile, 0)


def shards(nx, ny, adj, sig, elec):
    cx, cy, cz = sig.shape
    Z = cz // LANES
    current = math.sqrt(nx * cx * ny * cy * cz)
    block = jax.ShapeDtypeStruct(adj.shape, jnp.float32)
    hbm = pl.BlockSpec(memory_space=pltpu.HBM)
    vmem = pl.BlockSpec(memory_space=pltpu.VMEM)
    tall = cy + 2 * TILE
    f32 = lambda *dims: pltpu.VMEM(dims, jnp.float32)
    shape = lambda *dims: jax.ShapeDtypeStruct(dims, jnp.float32)
    dma = pltpu.SemaphoreType.DMA
    adj = pltpu.with_memory_space_constraint(adj, pltpu.HBM)
    sig = pltpu.with_memory_space_constraint(sig, pltpu.HBM)
    slots = max(Z // 2, 1)
    r, q, w, sums = pl.pallas_call(
        functools.partial(operator_kernel, nx, ny, current),
        out_shape=(
            shape(F, cx + 2, Z, tall, LANES), shape(F, cx, Z, tall, LANES), shape(F, cx, Z, cy, LANES),
            shape(TILE, LANES),
        ),
        in_specs=[hbm, hbm, pl.BlockSpec(memory_space=pltpu.SMEM)],
        out_specs=(vmem, vmem, vmem, vmem),
        scratch_shapes=[
            f32(cx + 2, Z, tall, LANES),
            f32(7, cx, Z, cy, LANES),
            f32(2, F, Z, cy, LANES),
            f32(slots, F, cy, LANES),
            f32(slots, cy, LANES),
            f32(slots, F, cy, LANES),
            f32(4 * NP, TILE, LANES),
            f32(nx, TILE, LANES),
            f32(ny, TILE, LANES),
            dma((2, Z)), dma((2, 3, Z)), dma((2, 3, Z)), dma((3, slots)), dma((3, slots)),
            dma((2, 5)), dma((2, 5)),
            dma((max(nx - 1, 1),)), dma((max(nx - 1, 1),)),
            dma((max(ny - 1, 1),)), dma((max(ny - 1, 1),)),
        ],
        compiler_params=pltpu.CompilerParams(collective_id=0, has_side_effects=True, vmem_limit_bytes=GRANT_A),
    )(adj, sig, elec)
    slab = pl.BlockSpec((F, 1, cy, cz), lambda x: (0, x, 0, 0))
    return pl.pallas_call(
        finish_kernel,
        grid=(cx,),
        out_shape=(block, block),
        in_specs=[vmem, vmem, vmem, vmem],
        out_specs=(slab, slab),
        scratch_shapes=[pltpu.VMEM((2 * F * F, LANES), jnp.float32)],
        compiler_params=pltpu.CompilerParams(vmem_limit_bytes=GRANT_B),
    )(sums, r, q, w)


def solution(mesh):
    placed = (P(None, "gx", "gy", None), P("gx", "gy", None), P())
    return jax.shard_map(
        functools.partial(shards, mesh.shape["gx"], mesh.shape["gy"]),
        mesh=mesh,
        in_specs=placed,
        out_specs=(P(None, "gx", "gy", None), P(None, "gx", "gy", None)),
        check_vma=False,
    )
```

time: 50.9 us -> 49.8 us (0.978)
  Pallas kernels: 49.5 us -> 48.4 us
    pallas_call x1, Pallas kernels: 42.1 us -> 40.8 us  [shards(): pl.pallas_call(functools.partial(operator_kernel, nx, ny, current), out_s...]
where the time goes in v1:
time: 49.8 us; the launch traced here: 49.7 us
  Pallas kernels  48.4 us (97%)
  local copies, waits for them, and re-layouts  0.65 us (1%)
  between operations  0.65 us (1%)
    pallas_call x1, Pallas kernels, shards(): pl.pallas_call(functools.partial(operator_kernel, nx, ny, current), out_s...  40.8 us
    pallas_call x1, Pallas kernels, shards(): pl.pallas_call(finish_kernel, grid=(cx,), out_shape=(block, block), in_sp...  7.57 us

profile of v1, /device:TPU:0, one launch (start us, length us, event | category | flops | bytes accessed | tf_op | source)
XLA Modules:
  0.0 49.7 jit_solution(7650813051401599387)
XLA Ops:
  0.6 0.0 copy-start
  0.6 0.6 %copy-done = s32[4]{0:T(128)S(1)} copy-done((s32[4]{0:T(128)S(1)}, s32[4]{0:T(128)}, u32[]{:S(2)}) %copy-start) | copy-done | bytes 40
  1.3 40.8 %shard_map.50 = (f32[4,10,4,80,128]{4,3,2,1,0:T(8,128)S(1)}, f32[4,8,4,80,128]{4,3,2,1,0:T(8,128)S(1)}, f32[4,8,4,64,128]{4,3,2,1,0:T(8,128)S(1)}, f32[8,128]{1,0:T(8,128)S(1)}) custom-call(f32[4,8,64,512]{3,2,1,0:T(8,128)} %adj.1, f32[8,64,512]{2,1,0:T(8,128)} %sig.1, s32[4]{0:T(128)S(1)} %copy-done), custom_call_target="tpu_custom_call" | custom-call | tf_op jit(solution)/shard_map/pallas_call | solution.py:580
  42.1 7.6 %shard_map.51 = (f32[4,8,64,512]{3,2,1,0:T(8,128)}, f32[4,8,64,512]{3,2,1,0:T(8,128)}) custom-call(f32[8,128]{1,0:T(8,128)S(1)} %get-tuple-element.6.sums, f32[4,10,4,80,128]{4,3,2,1,0:T(8,128)S(1)} %get-tuple-element.7.r_ref, f32[4,8,4,80,128]{4,3,2,1,0:T(8,128)S(1)} %get-tuple-element.8.q_ref, f32[4,8,4,64,128]{4,3,2,1,0:T(8,128)S(1)} %get-tuple-element.9.w_ref), custom_call_target="tpu_custom_call" | custom-call | tf_op jit(solution)/shard_map/pallas_call | solution.py:606
Async XLA Ops:
  0.6 0.7 %copy-start = (s32[4]{0:T(128)S(1)}, s32[4]{0:T(128)}, u32[]{:S(2)}) copy-start(s32[4]{0:T(128)} %elec.1) | copy-start | bytes 52

commit v2 on v1

--- a/solution.py
+++ b/solution.py
@@ -14,7 +14,7 @@
 NP = len(PAIRS)
 TILE = 8
 GRANT_A = 16 * 1024 * 1024
-GRANT_B = 5 * 1024 * 1024
+GRANT_B = 12 * 1024 * 1024
 LANES = 128
 
 
@@ -26,8 +26,8 @@
 
 
 def operator_kernel(
-    nx, ny, current, adj, sig, elec, R, Q, W, sums,
-    S, wt, qx, relay_r, relay_s, relay_q, acc, part_x, part_y,
+    nx, ny, current, adj, sig, elec_ref, R, Q, W, sums,
+    elec, S, wt, qx, relay_r, relay_q, acc, part_x, part_y,
     local, xs, xr, hr, fs, ys, yr, ax_s, ax_r, ay_s, ay_r,
 ):
     cx, cy, cz = sig.shape
@@ -39,32 +39,36 @@
     rows = pl.ds(TILE, cy)
     inner = pl.ds(1, cx)
 
-    loads = []
-    for z in range(Z):
-        at = pl.ds(z * LANES, LANES)
-        loads.append(pltpu.make_async_copy(adj.at[:, :, :, at], R.at[:, inner, z, rows, :], local.at[0, z]))
-        loads.append(pltpu.make_async_copy(sig.at[:, :, at], S.at[inner, z, rows, :], local.at[1, z]))
-    for load in loads:
-        load.start()
     for axis, me, n in (("gx", mx, nx), ("gy", my, ny)):
         for d in range(1, n):
             pl.semaphore_signal(
                 barrier, inc=1, device_id={axis: lax.rem(me + d, n)}, device_id_type=MESH
             )
 
+    loads = [pltpu.make_async_copy(elec_ref, elec, local.at[2])]
+    for z in range(Z):
+        at = pl.ds(z * LANES, LANES)
+        loads.append(pltpu.make_async_copy(adj.at[:, :, :, at], R.at[:, inner, z, rows, :], local.at[0]))
+        loads.append(pltpu.make_async_copy(sig.at[:, :, at], S.at[inner, z, rows, :], local.at[1]))
+    for load in loads:
+        load.start()
+
     has_lo, has_hi = mx > 0, mx < nx - 1
     below, above = jnp.maximum(mx - 1, 0), jnp.minimum(mx + 1, nx - 1)
     y_lo, y_hi = my > 0, my < ny - 1
     left, right = jnp.maximum(my - 1, 0), jnp.minimum(my + 1, ny - 1)
 
+    def take(ref, sem):
+        pltpu.make_async_copy(ref, ref, sem).wait()
+
     half = Z // 2
     mid = nx // 2
     relaying = nx >= 4
     order = [z for k in range(half) for z in (k, Z - 1 - k)] + ([half] if Z % 2 else [])
-    first_up = [z for z in order if z < half]
-    first_dn = [z for z in order if z >= half]
-    by_relay = [z for k, z in enumerate(order) if relaying and (k // 2) % 2 == 1]
-    slot = {z: k for k, z in enumerate(by_relay)}
+    first_up = [z for k, z in enumerate(order) if k % 4 in (0, 3)]
+    first_dn = [z for z in order if z not in first_up]
+    relay_0 = order[Z - half:] if relaying else []
+    relay_1 = order[:half] if relaying else []
     up_cross, dn_cross = mx == mid - 1, mx == mid
     up_end, dn_end = mx == nx - 1, mx == 0
 
@@ -75,62 +79,72 @@
         plane = cx - 1 if d == 0 else 0
         halo = 0 if d == 0 else cx + 1
         if k == 0:
-            src, dst = adj.at[:, plane, :, lanes(z)], R.at[:, halo, z, rows, :]
-        elif k == 1:
-            src, dst = sig.at[plane, :, lanes(z)], S.at[halo, z, rows, :]
+            pairs = [
+                (adj.at[:, plane, :, lanes(z)], R.at[:, halo, z, rows, :]),
+                (sig.at[plane, :, lanes(z)], S.at[halo, z, rows, :]),
+            ]
         else:
-            src, dst = Q.at[:, plane, z, rows, :], qx.at[d, :, z]
-        return remote(src, dst, xs.at[d, k, z], xr.at[d, k, z], "gx", axis_to)
+            pairs = [(Q.at[:, plane, z, rows, :], qx.at[d, :, z])]
+        return [remote(src, dst, xs.at[d], xr.at[d, k, z], "gx", axis_to) for src, dst in pairs]
 
     def to_relay(d, k, z):
         plane = cx - 1 if d == 0 else 0
         end = nx - 1 if d == 0 else 0
         if k == 0:
-            src = adj.at[:, plane, :, lanes(z)]
-        elif k == 1:
-            src = sig.at[plane, :, lanes(z)]
+            at = relay_0.index(z)
+            pairs = [
+                (adj.at[:, plane, :, lanes(z)], relay_r.at[at, pl.ds(0, F)]),
+                (sig.at[plane, :, lanes(z)], relay_r.at[at, F]),
+            ]
         else:
-            src = Q.at[:, plane, z, rows, :]
-        dst = (relay_r, relay_s, relay_q)[k].at[slot[z]]
-        return remote(src, dst, xs.at[d, k, z], hr.at[k, slot[z]], "gx", end)
+            at = relay_1.index(z)
+            pairs = [(Q.at[:, plane, z, rows, :], relay_q.at[at])]
+        return [remote(src, dst, xs.at[d], hr.at[k, at], "gx", end) for src, dst in pairs]
 
     def from_relay(d, k, z):
         halo = 0 if d == 0 else cx + 1
+        target = mid if d == 0 else mid - 1
         if k == 0:
-            dst = R.at[:, halo, z, rows, :]
-        elif k == 1:
-            dst = S.at[halo, z, rows, :]
+            at = relay_0.index(z)
+            pairs = [
+                (relay_r.at[at, pl.ds(0, F)], R.at[:, halo, z, rows, :]),
+                (relay_r.at[at, F], S.at[halo, z, rows, :]),
+            ]
         else:
-            dst = qx.at[d, :, z]
-        src = (relay_r, relay_s, relay_q)[k].at[slot[z]]
-        target = mid if d == 0 else mid - 1
-        return remote(src, dst, fs.at[k, slot[z]], xr.at[d, k, z], "gx", target)
+            pairs = [(relay_q.at[relay_1.index(z)], qx.at[d, :, z])]
+        return [remote(src, dst, fs.at[0], xr.at[d, k, z], "gx", target) for src, dst in pairs]
 
     sides = ((0, has_hi, above, up_cross, up_end), (1, has_lo, below, dn_cross, dn_end))
 
-    def send(d, k, z):
+    def start(copies):
+        for copy in copies:
+            copy.start()
+
+    def send_relayed(d, k, z):
+        if z in (relay_0, relay_1)[k]:
+            @pl.when(sides[d][3])
+            def _():
+                start(to_relay(d, k, z))
+
+    def send_direct(d, k, z):
         _, there, to, cross, _ = sides[d]
-        if z in by_relay:
-            @pl.when(there & jnp.logical_not(cross))
+        if z in (relay_0, relay_1)[k]:
+            there = there & jnp.logical_not(cross)
+
+        @pl.when(there)
+        def _():
+            start(hop(d, k, z, to))
+
+    def forward(d, k, z):
+        if z in (relay_0, relay_1)[k]:
+            @pl.when(sides[d][4])
             def _():
-                hop(d, k, z, to).start()
-
-            @pl.when(cross)
-            def _():
-                to_relay(d, k, z).start()
-        else:
-            @pl.when(there)
-            def _():
-                hop(d, k, z, to).start()
-
-    def forward(d, k, z):
-        @pl.when(sides[d][4])
-        def _():
-            to_relay(d, k, z).wait_recv()
-            from_relay(d, k, z).start()
+                at = (relay_0, relay_1)[k].index(z)
+                take((relay_r, relay_q)[k].at[at], hr.at[k, at])
+                start(from_relay(d, k, z))
 
     def arrive(d, k, z):
-        hop(d, k, z, above if d == 0 else below).wait_recv()
+        take((relay_r, relay_q)[k].at[0], xr.at[d, k, z])
 
     def y_hop(d, k):
         src_row, dst_row = (TILE + cy - 1, TILE - 1) if d == 0 else (TILE, TILE + cy)
@@ -145,7 +159,7 @@
         else:
             x = 0 if k == 3 else cx - 1
             src, dst = Q.at[:, x, :, src_row, :], Q.at[:, x, :, dst_row, :]
-        return remote(src, dst, ys.at[d, k], yr.at[d, k], "gy", to)
+        return remote(src, dst, ys.at[d], yr.at[d, k], "gy", to)
 
     def y_send(kinds):
         for d, there in ((0, y_hi), (1, y_lo)):
@@ -163,15 +177,18 @@
 
     pl.semaphore_wait(barrier, nx + ny - 2)
     for z in order:
-        for k in (0, 1):
-            send(0, k, z)
-            send(1, k, z)
+        for d in (0, 1):
+            send_relayed(d, 0, z)
+    for z in order:
+        for d in (0, 1):
+            send_direct(d, 0, z)
 
     acc[...] = jnp.zeros_like(acc)
     nothing = jnp.zeros((cy, LANES), jnp.float32)
     no_row = jnp.zeros((1, LANES), jnp.float32)
-    for load in loads:
-        load.wait()
+    take(W, local.at[0])
+    take(wt.at[0], local.at[1])
+    loads[0].wait()
 
     row_id = lax.broadcasted_iota(jnp.int32, (cy, LANES), 0)
     first = lax.broadcasted_iota(jnp.int32, (cy, LANES), 1) == 0
@@ -247,7 +264,7 @@
             acc[base + k] = acc[base + k] + total
 
     def first_tile(x, t, zs):
-        y = pl.multiple_of(t * TILE, TILE)
+        y = t * TILE
         at, up, dn = pl.ds(y + TILE, TILE), pl.ds(y + TILE - 1, TILE), pl.ds(y + TILE + 1, TILE)
         out_at = pl.ds(y, TILE)
         weights = {}
@@ -280,7 +297,7 @@
         add_grams(NP, rs, qs)
 
     def second_tile(x, t, zs, low, high):
-        y = pl.multiple_of(t * TILE, TILE)
+        y = t * TILE
         at, up, dn = pl.ds(y + TILE, TILE), pl.ds(y + TILE - 1, TILE), pl.ds(y + TILE + 1, TILE)
         out_at = pl.ds(y, TILE)
         qs, ws = [], []
@@ -320,86 +337,89 @@
     def face(d, z, grams):
         @pl.when((has_lo, has_hi)[d])
         def _():
-            arrive(d, 2, z)
+            arrive(d, 1, z)
             loop(0, T, lambda t: face_tile(d, z, t, grams))
 
     every = list(range(Z))
 
     def middle(planes, tile, *rest):
         lo, hi = planes
-        loop(lo, hi, lambda x: loop(1, T - 1, lambda t: tile(x, t, every, *rest)))
+        def plane(x):
+            for t in range(1, T - 1):
+                tile(x, t, every, *rest)
+        loop(lo, hi, plane)
 
     def rims(planes, tile, *rest):
         lo, hi = planes
-        loop(lo, hi, lambda x: loop(0, 2, lambda k: tile(x, k * (T - 1), every, *rest)))
+        def plane(x):
+            for t in (0, T - 1):
+                tile(x, t, every, *rest)
+        loop(lo, hi, plane)
 
     def chunk(z):
         for d, there in ((0, has_lo), (1, has_hi)):
             @pl.when(there)
             def _():
                 arrive(d, 0, z)
-                arrive(d, 1, z)
         if z == 0:
             loop(0, 2, lambda k: spike(k * (cx + 1)))
-        loop(0, 2, lambda k: loop(0, T, lambda t: first_tile(1 + k * (cx - 1), t, [z])))
-
-    def forward_all(k_list, zs):
+        def plane(k):
+            for t in range(T):
+                first_tile(1 + k * (cx - 1), t, [z])
+        loop(0, 2, plane)
+
+    def forward_all(k, zs, ds=(0, 1)):
         for z in zs:
-            for d in (0, 1):
-                for k in k_list:
-                    if z in by_relay:
-                        forward(d, k, z)
-
+            for d in ds:
+                forward(d, k, z)
+
+    def send_image(d, z):
+        send_relayed(d, 1, z)
+        send_direct(d, 1, z)
+
+    firsts = (first_up, first_dn)
+    late = [(d, z) for z in order for d in (0, 1) if z not in firsts[d]]
+    early = [(d, z) for z in order for d in (0, 1) if z in firsts[d]]
     split = (cx + 2) // 2
     middle((2, split), first_tile)
+    middle((split, cx), first_tile)
     y_arrive((0, 1))
-    forward_all((0, 1), by_relay[:1])
+    forward_all(0, relay_0[:1])
     rims((2, cx), first_tile)
-    forward_all((0, 1), by_relay[1:])
-    middle((split, cx), first_tile)
     y_send((2,))
-
-    sent_up = sent_dn = 0
-    ready = set()
-
-    def send_ready(d, limit):
-        plan = (first_up + first_dn) if d == 0 else (first_dn + first_up)
-        done = sent[d]
-        while len(done) < limit and plan[len(done)] in ready:
-            send(d, 2, plan[len(done)])
-            done.append(plan[len(done)])
-
-    sent = ([], [])
+    forward_all(0, relay_0[1:])
+    middle((3, cx - 1), second_tile, True, True)
     for n, z in enumerate(order):
-        chunk(z)
-        ready.add(z)
-        send_ready(0, Z)
-        send_ready(1, Z)
-        if n == 0:
-            middle((3, cx - 1), second_tile, True, True)
-        if n == 1:
+        if n == 2:
             y_arrive((2,))
             rims((3, cx - 1), second_tile, True, True)
+        if n == Z - 1:
+            for d in (0, 1):
+                forward_all(1, [c for c in relay_1[:1] if c in firsts[d]], (d,))
+        chunk(z)
+        for d in (0, 1):
+            if z in firsts[d]:
+                send_image(d, z)
+        if n == half - 1:
+            for d, c in late[:half]:
+                send_image(d, c)
     y_send((3, 4))
-
-    ends = lambda k: 2 + k * (cx - 3)
-    loop(0, 2, lambda k: loop(0, T, lambda t: second_tile(ends(k), t, every, True, True)))
+    for d in (0, 1):
+        forward_all(1, [c for c in relay_1[1:] if c in firsts[d]], (d,))
+
+    def beside_ends(k):
+        for t in range(T):
+            second_tile(2 + k * (cx - 3), t, every, True, True)
+    loop(0, 2, beside_ends)
     middle((1, 2), second_tile, False, True)
     middle((cx, cx + 1), second_tile, True, False)
     y_arrive((3, 4))
     rims((1, 2), second_tile, False, True)
     rims((cx, cx + 1), second_tile, True, False)
-
-    early = [(0, z) for z in first_up] + [(1, z) for z in first_dn]
-    late = [(0, z) for z in first_dn] + [(1, z) for z in first_up]
-    rank = {z: n for n, z in enumerate(order)}
-    early.sort(key=lambda p: rank[p[1]])
-    late.sort(key=lambda p: rank[p[1]])
-    for d, z in early:
-        if z in by_relay:
-            forward(d, 2, z)
     for d, z in early:
         face(d, z, True)
+    for d, z in late[:half]:
+        forward(d, 1, z)
 
     def compact(parts):
         lane_sum = jnp.sum(parts, axis=1, keepdims=True)
@@ -411,57 +431,46 @@
     part_x[mx] = compact(jnp.sum(acc[...], axis=1))
 
     def exchange(buf, axis, me, n, sends, recvs):
-        copies = [
-            remote(buf.at[me], buf.at[me], sends.at[d - 1], recvs.at[d - 1], axis, lax.rem(me + d, n))
-            for d in range(1, n)
-        ]
-        for copy in copies:
-            copy.start()
-        return copies
-
-    def gather(buf, axis, me, n, sends, recvs):
         for d in range(1, n):
-            src = lax.rem(me + n - d, n)
-            remote(
-                buf.at[me], buf.at[src], sends.at[d - 1], recvs.at[d - 1], axis, src
-            ).wait_recv()
+            remote(buf.at[me], buf.at[me], sends.at[0], recvs.at[0], axis, lax.rem(me + d, n)).start()
+
+    def gather(buf, n, recvs):
+        if n > 1:
+            take(buf.at[pl.ds(0, n - 1)], recvs.at[0])
         total = buf[0]
         for k in range(1, n):
             total = total + buf[k]
         return total
 
-    copies_x = exchange(part_x, "gx", mx, nx, ax_s, ax_r)
+    exchange(part_x, "gx", mx, nx, ax_s, ax_r)
+    for d, z in late[half:]:
+        send_image(d, z)
+    part_y[my] = gather(part_x, nx, ax_r)
+    exchange(part_y, "gy", my, ny, ay_s, ay_r)
+    for d, z in late[half:]:
+        forward(d, 1, z)
     for d, z in late:
-        if z in by_relay:
-            forward(d, 2, z)
-    cut = len(late) // 2
-    for d, z in late[:cut]:
         face(d, z, False)
-    part_y[my] = gather(part_x, "gx", mx, nx, ax_s, ax_r)
-    copies_y = exchange(part_y, "gy", my, ny, ay_s, ay_r)
-    for d, z in late[cut:]:
-        face(d, z, False)
-    sums[...] = gather(part_y, "gy", my, ny, ay_s, ay_r)
-
-    for copy in copies_x + copies_y:
-        copy.wait_send()
+    sums[...] = gather(part_y, ny, ay_r)
+
+    if nx > 1:
+        take(part_x.at[pl.ds(0, nx - 1)], ax_s.at[0])
+    if ny > 1:
+        take(part_y.at[pl.ds(0, ny - 1)], ay_s.at[0])
+    three = pl.ds(0, 3)
     for d in (0, 1):
         @pl.when(sides[d][1])
         def _():
-            for z in order:
-                for k in range(3):
-                    hop(d, k, z, sides[d][2]).wait_send()
-
-        @pl.when(sides[d][4])
+            take(wt.at[three, three], xs.at[d])
+
+        @pl.when((y_hi, y_lo)[d])
         def _():
-            for z in by_relay:
-                for k in range(3):
-                    from_relay(d, k, z).wait_send()
-    for d, there in ((0, y_hi), (1, y_lo)):
-        @pl.when(there)
+            take(wt.at[0, :, :, pl.ds(0, 2 * F + 1), :], ys.at[d])
+
+    if relaying:
+        @pl.when(up_end | dn_end)
         def _():
-            for k in range(5):
-                y_hop(d, k).wait_send()
+            take(wt.at[three, three, pl.ds(0, half)], fs.at[0])
 
 
 def mat(a, b):
@@ -505,9 +514,8 @@
     return out
 
 
-def finish_kernel(sums, r_ref, q_ref, w_ref, x_ref, e_ref, coef):
-    @pl.when(pl.program_id(0) == 0)
-    def _():
+def finish_kernel(sums, r_ref, q_ref, w_ref, x_out, e_out, x_ref, e_ref, coef, sems):
+    def prepare():
         lane = lax.broadcasted_iota(jnp.int32, (TILE, LANES), 1)
         rows = []
         for k in range(4 * NP // TILE):
@@ -531,36 +539,77 @@
         a1 = spd_solve(curve, rr)
         m1 = add(add(a0, a1), mat(beta, a1))
         m2 = mat(a0, a1)
-        for i in range(F):
+        zero = jnp.zeros_like(m1[0][0])
+        one = zero + 1.0
+        weights = []
+        for j in range(F):
+            weights.append([m1[i][j] + m1[i][j] for i in range(F)] + [-(m2[i][j] + m2[i][j]) for i in range(F)] + [zero] * F)
+        for j in range(F):
+            unit = [one if i == j else zero for i in range(F)]
+            weights.append(unit + [-m1[i][j] for i in range(F)] + [m2[i][j] for i in range(F)])
+        depth = 3 * F * TILE
+        row_s = lax.broadcasted_iota(jnp.int32, (TILE, LANES), 0)
+        blocks = [[None] * 2 for _ in weights]
+        for h in range(2):
+            column = lane + h * LANES
+            column = jnp.where(column >= depth, column - depth, column)
+            at = [column == k * TILE + row_s for k in range(3 * F)]
+            for j, row in enumerate(weights):
+                block = jnp.zeros((TILE, LANES), jnp.float32)
+                for k in range(3 * F):
+                    if row[k] is not zero:
+                        block = jnp.where(at[k], jnp.broadcast_to(row[k], block.shape), block)
+                blocks[j][h] = block
+        full = jnp.concatenate([jnp.concatenate(pair, axis=1) for pair in blocks], axis=0)[:, :2 * depth]
+        high = full.astype(jnp.bfloat16)
+        low = (full - high.astype(jnp.float32)).astype(jnp.bfloat16)
+        coef[...] = jnp.concatenate([high, low], axis=0)
+
+    prepare()
+    cx, Z, cy = w_ref.shape[1:4]
+    wide = 2 if Z % 2 == 0 else 1
+
+    def tile(x, t):
+        y, wide_y = pl.ds(t * TILE, TILE), pl.ds(t * TILE + TILE, TILE)
+        for z in range(0, Z, wide):
+            stack = []
+            for n in range(z, z + wide):
+                stack.append(jnp.concatenate(
+                    [r_ref[f, x + 1, n, wide_y, :] for f in range(F)]
+                    + [q_ref[f, x, n, wide_y, :] for f in range(F)]
+                    + [w_ref[f, x, n, y, :] for f in range(F)], axis=0))
+            fields = jnp.concatenate(stack, axis=1)
+            high = fields.astype(jnp.bfloat16)
+            low = (fields - high.astype(jnp.float32)).astype(jnp.bfloat16)
+            both = jnp.concatenate([high, low], axis=0)
+            out = jnp.dot(coef[...], both, preferred_element_type=jnp.float32)
+            n_out = 2 * F * TILE
+            out = out[:n_out] + out[n_out:]
+            at = pl.ds(z * LANES, wide * LANES)
             for j in range(F):
-                coef[pl.ds(i * F + j, 1), :] = m1[i][j]
-                coef[pl.ds(F * F + i * F + j, 1), :] = m2[i][j]
-
-    x = pl.program_id(0)
-    cy = w_ref.shape[3]
-    Z = w_ref.shape[2]
-    c1 = [[jnp.broadcast_to(coef[pl.ds(i * F + j, 1), :], (TILE, LANES)) for j in range(F)] for i in range(F)]
-    c2 = [[jnp.broadcast_to(coef[pl.ds(F * F + i * F + j, 1), :], (TILE, LANES)) for j in range(F)] for i in range(F)]
-
-    def tile(t, c):
-        y = pl.ds(pl.multiple_of(t * TILE, TILE), TILE)
-        wide_y = pl.ds(pl.multiple_of(t * TILE + TILE, TILE), TILE)
-        for z in range(Z):
-            at = pl.ds(z * LANES, LANES)
-            rs = [r_ref[f, x + 1, z, wide_y, :] for f in range(F)]
-            qs = [q_ref[f, x, z, wide_y, :] for f in range(F)]
-            ws = [w_ref[f, x, z, y, :] for f in range(F)]
-            for j in range(F):
-                field = rs[0] * c1[0][j] - qs[0] * c2[0][j]
-                left = rs[j] - qs[0] * c1[0][j] + ws[0] * c2[0][j]
-                for i in range(1, F):
-                    field = field + rs[i] * c1[i][j] - qs[i] * c2[i][j]
-                    left = left - qs[i] * c1[i][j] + ws[i] * c2[i][j]
-                x_ref[j, 0, y, at] = field + field
-                e_ref[j, 0, y, at] = left
+                x_ref[j, x, y, at] = out[j * TILE:(j + 1) * TILE]
+                e_ref[j, x, y, at] = out[(F + j) * TILE:(F + j + 1) * TILE]
+
+    def out_copies(x):
+        return (
+            pltpu.make_async_copy(x_ref.at[:, x], x_out.at[:, x], sems.at[0, x]),
+            pltpu.make_async_copy(e_ref.at[:, x], e_out.at[:, x], sems.at[1, x]),
+        )
+
+    def plane(x, c):
+        for t in range(cy // TILE):
+            tile(x, t)
+        for copy in out_copies(x):
+            copy.start()
         return c
 
-    lax.fori_loop(0, cy // TILE, tile, 0)
+    def finish(x, c):
+        for copy in out_copies(x):
+            copy.wait()
+        return c
+
+    lax.fori_loop(0, cx, plane, 0)
+    lax.fori_loop(0, cx, finish, 0)
 
 
 def shards(nx, ny, adj, sig, elec):
@@ -576,6 +625,7 @@
     dma = pltpu.SemaphoreType.DMA
     adj = pltpu.with_memory_space_constraint(adj, pltpu.HBM)
     sig = pltpu.with_memory_space_constraint(sig, pltpu.HBM)
+    elec = pltpu.with_memory_space_constraint(elec, pltpu.HBM)
     slots = max(Z // 2, 1)
     r, q, w, sums = pl.pallas_call(
         functools.partial(operator_kernel, nx, ny, current),
@@ -583,33 +633,34 @@
             shape(F, cx + 2, Z, tall, LANES), shape(F, cx, Z, tall, LANES), shape(F, cx, Z, cy, LANES),
             shape(TILE, LANES),
         ),
-        in_specs=[hbm, hbm, pl.BlockSpec(memory_space=pltpu.SMEM)],
+        in_specs=[hbm, hbm, hbm],
         out_specs=(vmem, vmem, vmem, vmem),
         scratch_shapes=[
+            pltpu.SMEM((F,), jnp.int32),
             f32(cx + 2, Z, tall, LANES),
             f32(7, cx, Z, cy, LANES),
             f32(2, F, Z, cy, LANES),
-            f32(slots, F, cy, LANES),
-            f32(slots, cy, LANES),
+            f32(slots, F + 1, cy, LANES),
             f32(slots, F, cy, LANES),
             f32(4 * NP, TILE, LANES),
             f32(nx, TILE, LANES),
             f32(ny, TILE, LANES),
-            dma((2, Z)), dma((2, 3, Z)), dma((2, 3, Z)), dma((3, slots)), dma((3, slots)),
-            dma((2, 5)), dma((2, 5)),
-            dma((max(nx - 1, 1),)), dma((max(nx - 1, 1),)),
-            dma((max(ny - 1, 1),)), dma((max(ny - 1, 1),)),
+            dma((3,)), dma((2,)), dma((2, 2, Z)), dma((2, slots)), dma((1,)),
+            dma((2,)), dma((2, 5)),
+            dma((1,)), dma((1,)), dma((1,)), dma((1,)),
         ],
         compiler_params=pltpu.CompilerParams(collective_id=0, has_side_effects=True, vmem_limit_bytes=GRANT_A),
     )(adj, sig, elec)
-    slab = pl.BlockSpec((F, 1, cy, cz), lambda x: (0, x, 0, 0))
     return pl.pallas_call(
         finish_kernel,
-        grid=(cx,),
         out_shape=(block, block),
         in_specs=[vmem, vmem, vmem, vmem],
-        out_specs=(slab, slab),
-        scratch_shapes=[pltpu.VMEM((2 * F * F, LANES), jnp.float32)],
+        out_specs=(hbm, hbm),
+        scratch_shapes=[
+            f32(F, cx, cy, cz), f32(F, cx, cy, cz),
+            pltpu.VMEM((4 * F * TILE, 6 * F * TILE), jnp.bfloat16),
+            dma((2, cx)),
+        ],
         compiler_params=pltpu.CompilerParams(vmem_limit_bytes=GRANT_B),
     )(sums, r, q, w)
 

time: 49.8 us -> 37.6 us (0.76)
  Pallas kernels: 48.4 us -> 36.8 us
  local copies, waits for them, and re-layouts: 0.65 us -> 0 us
    pallas_call x1, Pallas kernels: 40.8 us -> 31.6 us  [shards(): pl.pallas_call(functools.partial(operator_kernel, nx, ny, current), out_s...]
    pallas_call x1, Pallas kernels: 7.57 us -> 5.21 us  [shards(): pl.pallas_call(finish_kernel, out_shape=(block, block), in_specs=[vmem, v...]
    unnamed x2 -> x0, local copies, waits for them, and re-layouts: 0.65 us -> none
where the time goes in v2:
time: 37.6 us; the launch traced here: 37.5 us
  Pallas kernels  36.8 us (98%)
  between operations  0.64 us (2%)
    pallas_call x1, Pallas kernels, shards(): pl.pallas_call(functools.partial(operator_kernel, nx, ny, current), out_s...  31.6 us
    pallas_call x1, Pallas kernels, shards(): pl.pallas_call(finish_kernel, out_shape=(block, block), in_specs=[vmem, v...  5.21 us

profile of v2, /device:TPU:0, one launch (start us, length us, event | category | flops | bytes accessed | tf_op | source)
XLA Modules:
  0.0 37.5 jit_solution(15720330984610347825)
XLA Ops:
  0.6 31.6 %shard_map.50 = (f32[4,10,4,80,128]{4,3,2,1,0:T(8,128)S(1)}, f32[4,8,4,80,128]{4,3,2,1,0:T(8,128)S(1)}, f32[4,8,4,64,128]{4,3,2,1,0:T(8,128)S(1)}, f32[8,128]{1,0:T(8,128)S(1)}) custom-call(f32[4,8,64,512]{3,2,1,0:T(8,128)} %adj.1, f32[8,64,512]{2,1,0:T(8,128)} %sig.1, s32[4]{0:T(128)} %elec_ref.1), custom_call_target="tpu_custom_call" | custom-call | tf_op jit(solution)/shard_map/pallas_call | solution.py:630
  32.3 5.2 %shard_map.51 = (f32[4,8,64,512]{3,2,1,0:T(8,128)}, f32[4,8,64,512]{3,2,1,0:T(8,128)}) custom-call(f32[8,128]{1,0:T(8,128)S(1)} %get-tuple-element.6.sums, f32[4,10,4,80,128]{4,3,2,1,0:T(8,128)S(1)} %get-tuple-element.7.r_ref, f32[4,8,4,80,128]{4,3,2,1,0:T(8,128)S(1)} %get-tuple-element.8.q_ref, f32[4,8,4,64,128]{4,3,2,1,0:T(8,128)S(1)} %get-tuple-element.9.w_ref), custom_call_target="tpu_custom_call" | custom-call | tf_op jit(solution)/shard_map/pallas_call | solution.py:654

commit v3 on v2

--- a/solution.py
+++ b/solution.py
@@ -85,7 +85,7 @@
             ]
         else:
             pairs = [(Q.at[:, plane, z, rows, :], qx.at[d, :, z])]
-        return [remote(src, dst, xs.at[d], xr.at[d, k, z], "gx", axis_to) for src, dst in pairs]
+        return [remote(src, dst, xs.at[d, k], xr.at[d, k, z], "gx", axis_to) for src, dst in pairs]
 
     def to_relay(d, k, z):
         plane = cx - 1 if d == 0 else 0
@@ -99,7 +99,7 @@
         else:
             at = relay_1.index(z)
             pairs = [(Q.at[:, plane, z, rows, :], relay_q.at[at])]
-        return [remote(src, dst, xs.at[d], hr.at[k, at], "gx", end) for src, dst in pairs]
+        return [remote(src, dst, xs.at[d, k], hr.at[k, at], "gx", end) for src, dst in pairs]
 
     def from_relay(d, k, z):
         halo = 0 if d == 0 else cx + 1
@@ -112,7 +112,7 @@
             ]
         else:
             pairs = [(relay_q.at[relay_1.index(z)], qx.at[d, :, z])]
-        return [remote(src, dst, fs.at[0], xr.at[d, k, z], "gx", target) for src, dst in pairs]
+        return [remote(src, dst, fs.at[k], xr.at[d, k, z], "gx", target) for src, dst in pairs]
 
     sides = ((0, has_hi, above, up_cross, up_end), (1, has_lo, below, dn_cross, dn_end))
 
@@ -373,10 +373,6 @@
             for d in ds:
                 forward(d, k, z)
 
-    def send_image(d, z):
-        send_relayed(d, 1, z)
-        send_direct(d, 1, z)
-
     firsts = (first_up, first_dn)
     late = [(d, z) for z in order for d in (0, 1) if z not in firsts[d]]
     early = [(d, z) for z in order for d in (0, 1) if z in firsts[d]]
@@ -395,31 +391,37 @@
             rims((3, cx - 1), second_tile, True, True)
         if n == Z - 1:
             for d in (0, 1):
-                forward_all(1, [c for c in relay_1[:1] if c in firsts[d]], (d,))
+                @pl.when(sides[d][1])
+                def _():
+                    take(wt.at[0, pl.ds(0, F + 1)], xs.at[d, 0])
+                for c in order[:n]:
+                    if c in firsts[d]:
+                        send_direct(d, 1, c)
         chunk(z)
         for d in (0, 1):
-            if z in firsts[d]:
-                send_image(d, z)
-        if n == half - 1:
-            for d, c in late[:half]:
-                send_image(d, c)
+            send_relayed(d, 1, z)
+    for d in (0, 1):
+        if order[Z - 1] in firsts[d]:
+            send_direct(d, 1, order[Z - 1])
+    for d, c in late[:half]:
+        send_direct(d, 1, c)
     y_send((3, 4))
-    for d in (0, 1):
-        forward_all(1, [c for c in relay_1[1:] if c in firsts[d]], (d,))
 
     def beside_ends(k):
         for t in range(T):
             second_tile(2 + k * (cx - 3), t, every, True, True)
     loop(0, 2, beside_ends)
+    for d, z in early:
+        forward(d, 1, z)
     middle((1, 2), second_tile, False, True)
     middle((cx, cx + 1), second_tile, True, False)
     y_arrive((3, 4))
     rims((1, 2), second_tile, False, True)
     rims((cx, cx + 1), second_tile, True, False)
+    for d, z in late[:half]:
+        forward(d, 1, z)
     for d, z in early:
         face(d, z, True)
-    for d, z in late[:half]:
-        forward(d, 1, z)
 
     def compact(parts):
         lane_sum = jnp.sum(parts, axis=1, keepdims=True)
@@ -444,7 +446,7 @@
 
     exchange(part_x, "gx", mx, nx, ax_s, ax_r)
     for d, z in late[half:]:
-        send_image(d, z)
+        send_direct(d, 1, z)
     part_y[my] = gather(part_x, nx, ax_r)
     exchange(part_y, "gy", my, ny, ay_s, ay_r)
     for d, z in late[half:]:
@@ -457,20 +459,20 @@
         take(part_x.at[pl.ds(0, nx - 1)], ax_s.at[0])
     if ny > 1:
         take(part_y.at[pl.ds(0, ny - 1)], ay_s.at[0])
-    three = pl.ds(0, 3)
     for d in (0, 1):
         @pl.when(sides[d][1])
         def _():
-            take(wt.at[three, three], xs.at[d])
+            take(W.at[0, pl.ds(0, F)], xs.at[d, 1])
 
         @pl.when((y_hi, y_lo)[d])
         def _():
             take(wt.at[0, :, :, pl.ds(0, 2 * F + 1), :], ys.at[d])
 
-    if relaying:
+    if relay_0 and relay_1:
         @pl.when(up_end | dn_end)
         def _():
-            take(wt.at[three, three, pl.ds(0, half)], fs.at[0])
+            take(relay_r.at[pl.ds(0, len(relay_0))], fs.at[0])
+            take(relay_q.at[pl.ds(0, len(relay_1))], fs.at[1])
 
 
 def mat(a, b):
@@ -590,26 +592,29 @@
                 x_ref[j, x, y, at] = out[j * TILE:(j + 1) * TILE]
                 e_ref[j, x, y, at] = out[(F + j) * TILE:(F + j + 1) * TILE]
 
-    def out_copies(x):
+    parts = 2 if cy % (2 * TILE) == 0 else 1
+    part = cy // parts
+
+    def out_copies(x, h):
+        y = pl.ds(h * part, part)
         return (
-            pltpu.make_async_copy(x_ref.at[:, x], x_out.at[:, x], sems.at[0, x]),
-            pltpu.make_async_copy(e_ref.at[:, x], e_out.at[:, x], sems.at[1, x]),
+            pltpu.make_async_copy(x_ref.at[:, x, y], x_out.at[:, x, y], sems.at[0, x, h]),
+            pltpu.make_async_copy(e_ref.at[:, x, y], e_out.at[:, x, y], sems.at[1, x, h]),
         )
 
     def plane(x, c):
-        for t in range(cy // TILE):
-            tile(x, t)
-        for copy in out_copies(x):
-            copy.start()
+        for h in range(parts):
+            for t in range(h * part // TILE, (h + 1) * part // TILE):
+                tile(x, t)
+            for copy in out_copies(x, h):
+                copy.start()
         return c
 
-    def finish(x, c):
-        for copy in out_copies(x):
-            copy.wait()
-        return c
-
     lax.fori_loop(0, cx, plane, 0)
-    lax.fori_loop(0, cx, finish, 0)
+    for x in range(cx):
+        for h in range(parts):
+            for copy in out_copies(x, h):
+                copy.wait()
 
 
 def shards(nx, ny, adj, sig, elec):
@@ -645,7 +650,7 @@
             f32(4 * NP, TILE, LANES),
             f32(nx, TILE, LANES),
             f32(ny, TILE, LANES),
-            dma((3,)), dma((2,)), dma((2, 2, Z)), dma((2, slots)), dma((1,)),
+            dma((3,)), dma((2, 2)), dma((2, 2, Z)), dma((2, slots)), dma((2,)),
             dma((2,)), dma((2, 5)),
             dma((1,)), dma((1,)), dma((1,)), dma((1,)),
         ],
@@ -659,7 +664,7 @@
         scratch_shapes=[
             f32(F, cx, cy, cz), f32(F, cx, cy, cz),
             pltpu.VMEM((4 * F * TILE, 6 * F * TILE), jnp.bfloat16),
-            dma((2, cx)),
+            dma((2, cx, 2)),
         ],
         compiler_params=pltpu.CompilerParams(vmem_limit_bytes=GRANT_B),
     )(sums, r, q, w)

time: 37.6 us -> 36.7 us (0.976)
  Pallas kernels: 36.8 us -> 36 us
    pallas_call x1, Pallas kernels: 31.6 us -> 30.8 us  [shards(): pl.pallas_call(functools.partial(operator_kernel, nx, ny, current), out_s...]
where the time goes in v3:
time: 36.7 us; the launch traced here: 36.6 us
  Pallas kernels  36 us (98%)
  between operations  0.64 us (2%)
    pallas_call x1, Pallas kernels, shards(): pl.pallas_call(functools.partial(operator_kernel, nx, ny, current), out_s...  30.8 us
    pallas_call x1, Pallas kernels, shards(): pl.pallas_call(finish_kernel, out_shape=(block, block), in_specs=[vmem, v...  5.18 us

profile of v3, /device:TPU:0, one launch (start us, length us, event | category | flops | bytes accessed | tf_op | source)
XLA Modules:
  0.0 36.6 jit_solution(11586337485222146745)
XLA Ops:
  0.6 30.8 %shard_map.50 = (f32[4,10,4,80,128]{4,3,2,1,0:T(8,128)S(1)}, f32[4,8,4,80,128]{4,3,2,1,0:T(8,128)S(1)}, f32[4,8,4,64,128]{4,3,2,1,0:T(8,128)S(1)}, f32[8,128]{1,0:T(8,128)S(1)}) custom-call(f32[4,8,64,512]{3,2,1,0:T(8,128)} %adj.1, f32[8,64,512]{2,1,0:T(8,128)} %sig.1, s32[4]{0:T(128)} %elec_ref.1), custom_call_target="tpu_custom_call" | custom-call | tf_op jit(solution)/shard_map/pallas_call | solution.py:635
  31.4 5.2 %shard_map.51 = (f32[4,8,64,512]{3,2,1,0:T(8,128)}, f32[4,8,64,512]{3,2,1,0:T(8,128)}) custom-call(f32[8,128]{1,0:T(8,128)S(1)} %get-tuple-element.6.sums, f32[4,10,4,80,128]{4,3,2,1,0:T(8,128)S(1)} %get-tuple-element.7.r_ref, f32[4,8,4,80,128]{4,3,2,1,0:T(8,128)S(1)} %get-tuple-element.8.q_ref, f32[4,8,4,64,128]{4,3,2,1,0:T(8,128)S(1)} %get-tuple-element.9.w_ref), custom_call_target="tpu_custom_call" | custom-call | tf_op jit(solution)/shard_map/pallas_call | solution.py:659

commit v4 on v3

--- a/solution.py
+++ b/solution.py
@@ -67,7 +67,7 @@
     order = [z for k in range(half) for z in (k, Z - 1 - k)] + ([half] if Z % 2 else [])
     first_up = [z for k, z in enumerate(order) if k % 4 in (0, 3)]
     first_dn = [z for z in order if z not in first_up]
-    relay_0 = order[Z - half:] if relaying else []
+    relay_0 = order[1::2] if relaying else []
     relay_1 = order[:half] if relaying else []
     up_cross, dn_cross = mx == mid - 1, mx == mid
     up_end, dn_end = mx == nx - 1, mx == 0
@@ -403,8 +403,6 @@
     for d in (0, 1):
         if order[Z - 1] in firsts[d]:
             send_direct(d, 1, order[Z - 1])
-    for d, c in late[:half]:
-        send_direct(d, 1, c)
     y_send((3, 4))
 
     def beside_ends(k):
@@ -418,8 +416,6 @@
     y_arrive((3, 4))
     rims((1, 2), second_tile, False, True)
     rims((cx, cx + 1), second_tile, True, False)
-    for d, z in late[:half]:
-        forward(d, 1, z)
     for d, z in early:
         face(d, z, True)
 
@@ -445,7 +441,9 @@
         return total
 
     exchange(part_x, "gx", mx, nx, ax_s, ax_r)
-    for d, z in late[half:]:
+    for d, z in late[:half]:
+        forward(d, 1, z)
+    for d, z in late:
         send_direct(d, 1, z)
     part_y[my] = gather(part_x, nx, ax_r)
     exchange(part_y, "gy", my, ny, ay_s, ay_r)

time: 36.7 us -> 36.7 us (level)
  no operation moved by 1% of the time
where the time goes in v4:
time: 36.7 us; the launch traced here: 36.6 us
  Pallas kernels  35.9 us (98%)
  between operations  0.64 us (2%)
    pallas_call x1, Pallas kernels, shards(): pl.pallas_call(functools.partial(operator_kernel, nx, ny, current), out_s...  30.8 us
    pallas_call x1, Pallas kernels, shards(): pl.pallas_call(finish_kernel, out_shape=(block, block), in_specs=[vmem, v...  5.18 us

profile of v4, /device:TPU:0, one launch (start us, length us, event | category | flops | bytes accessed | tf_op | source)
XLA Modules:
  0.0 36.6 jit_solution(17975612724013443832)
XLA Ops:
  0.6 30.8 %shard_map.50 = (f32[4,10,4,80,128]{4,3,2,1,0:T(8,128)S(1)}, f32[4,8,4,80,128]{4,3,2,1,0:T(8,128)S(1)}, f32[4,8,4,64,128]{4,3,2,1,0:T(8,128)S(1)}, f32[8,128]{1,0:T(8,128)S(1)}) custom-call(f32[4,8,64,512]{3,2,1,0:T(8,128)} %adj.1, f32[8,64,512]{2,1,0:T(8,128)} %sig.1, s32[4]{0:T(128)} %elec_ref.1), custom_call_target="tpu_custom_call" | custom-call | tf_op jit(solution)/shard_map/pallas_call | solution.py:633
  31.4 5.2 %shard_map.51 = (f32[4,8,64,512]{3,2,1,0:T(8,128)}, f32[4,8,64,512]{3,2,1,0:T(8,128)}) custom-call(f32[8,128]{1,0:T(8,128)S(1)} %get-tuple-element.6.sums, f32[4,10,4,80,128]{4,3,2,1,0:T(8,128)S(1)} %get-tuple-element.7.r_ref, f32[4,8,4,80,128]{4,3,2,1,0:T(8,128)S(1)} %get-tuple-element.8.q_ref, f32[4,8,4,64,128]{4,3,2,1,0:T(8,128)S(1)} %get-tuple-element.9.w_ref), custom_call_target="tpu_custom_call" | custom-call | tf_op jit(solution)/shard_map/pallas_call | solution.py:657

commit v5 on v3

--- a/solution.py
+++ b/solution.py
@@ -592,14 +592,14 @@
                 x_ref[j, x, y, at] = out[j * TILE:(j + 1) * TILE]
                 e_ref[j, x, y, at] = out[(F + j) * TILE:(F + j + 1) * TILE]
 
-    parts = 2 if cy % (2 * TILE) == 0 else 1
+    parts = 4 if cy % (4 * TILE) == 0 else 1
     part = cy // parts
 
     def out_copies(x, h):
         y = pl.ds(h * part, part)
         return (
-            pltpu.make_async_copy(x_ref.at[:, x, y], x_out.at[:, x, y], sems.at[0, x, h]),
-            pltpu.make_async_copy(e_ref.at[:, x, y], e_out.at[:, x, y], sems.at[1, x, h]),
+            pltpu.make_async_copy(x_ref.at[:, x, y], x_out.at[:, x, y], sems.at[0]),
+            pltpu.make_async_copy(e_ref.at[:, x, y], e_out.at[:, x, y], sems.at[1]),
         )
 
     def plane(x, c):
@@ -611,10 +611,8 @@
         return c
 
     lax.fori_loop(0, cx, plane, 0)
-    for x in range(cx):
-        for h in range(parts):
-            for copy in out_copies(x, h):
-                copy.wait()
+    pltpu.make_async_copy(x_ref, x_out, sems.at[0]).wait()
+    pltpu.make_async_copy(e_ref, e_out, sems.at[1]).wait()
 
 
 def shards(nx, ny, adj, sig, elec):
@@ -664,7 +662,7 @@
         scratch_shapes=[
             f32(F, cx, cy, cz), f32(F, cx, cy, cz),
             pltpu.VMEM((4 * F * TILE, 6 * F * TILE), jnp.bfloat16),
-            dma((2, cx, 2)),
+            dma((2,)),
         ],
         compiler_params=pltpu.CompilerParams(vmem_limit_bytes=GRANT_B),
     )(sums, r, q, w)

time: 36.7 us -> 36.4 us (level)
  Pallas kernels: 36 us -> 35.6 us
where the time goes in v5:
time: 36.4 us; the launch traced here: 36.3 us
  Pallas kernels  35.6 us (98%)
  between operations  0.64 us (2%)
    pallas_call x1, Pallas kernels, shards(): pl.pallas_call(functools.partial(operator_kernel, nx, ny, current), out_s...  30.8 us
    pallas_call x1, Pallas kernels, shards(): pl.pallas_call(finish_kernel, out_shape=(block, block), in_specs=[vmem, v...  4.84 us

profile of v5, /device:TPU:0, one launch (start us, length us, event | category | flops | bytes accessed | tf_op | source)
XLA Modules:
  0.0 36.3 jit_solution(252995112714911617)
XLA Ops:
  0.6 30.8 %shard_map.50 = (f32[4,10,4,80,128]{4,3,2,1,0:T(8,128)S(1)}, f32[4,8,4,80,128]{4,3,2,1,0:T(8,128)S(1)}, f32[4,8,4,64,128]{4,3,2,1,0:T(8,128)S(1)}, f32[8,128]{1,0:T(8,128)S(1)}) custom-call(f32[4,8,64,512]{3,2,1,0:T(8,128)} %adj.1, f32[8,64,512]{2,1,0:T(8,128)} %sig.1, s32[4]{0:T(128)} %elec_ref.1), custom_call_target="tpu_custom_call" | custom-call | tf_op jit(solution)/shard_map/pallas_call | solution.py:633
  31.4 4.8 %shard_map.51 = (f32[4,8,64,512]{3,2,1,0:T(8,128)}, f32[4,8,64,512]{3,2,1,0:T(8,128)}) custom-call(f32[8,128]{1,0:T(8,128)S(1)} %get-tuple-element.6.sums, f32[4,10,4,80,128]{4,3,2,1,0:T(8,128)S(1)} %get-tuple-element.7.r_ref, f32[4,8,4,80,128]{4,3,2,1,0:T(8,128)S(1)} %get-tuple-element.8.q_ref, f32[4,8,4,64,128]{4,3,2,1,0:T(8,128)S(1)} %get-tuple-element.9.w_ref), custom_call_target="tpu_custom_call" | custom-call | tf_op jit(solution)/shard_map/pallas_call | solution.py:657
